TPU v7x, 256 devices: a whole 4x4x8 slice. The times are simulated.
256 devices in a mesh: bank: 128 (over y, z, x), sub: 2 (over core).
Axes of the slice: x: 4, y: 4, z: 8, core: 2. Of those that a mesh axis runs over, the one named last changes fastest.
Arguments:
- embeddings: bfloat16 [786432, 1024], P(('bank', 'sub'))
- pivots: int32 [2, 256], replicated, may hold values from 0 to 786431, as said below
Outputs:
- basis: float32 [786432, 512], P(('bank', 'sub'))
- triangle: float32 [512, 512], replicated
Inputs may be any that keep to these rules, and one draw needn't show every extreme that they name: All 512 entries are distinct molecules. Molecule g lies on device g // 3072 of bank+sub (bank slowest). Each device holds at most 1 pivots of each block step, and some device holds exactly 1.
All inputs are finite; a program needn't handle non-finite values.
Results may differ from a plain program's by a relative error of at most 0.0003.
Values may be sent and summed in bfloat16 or wider, within the bound.
A program may use at most 64 MiB of HBM per device.

v0:
```python
import jax
import jax.numpy as jnp
from jax import lax
from jax.sharding import PartitionSpec as P

P_SIZE = 256


def lower_inverse(factor):
    identity = jnp.eye(factor.shape[0], dtype=factor.dtype)
    return lax.linalg.triangular_solve(factor, identity, left_side=True, lower=True)


def times_transposed(left, right, exact):
    if exact:
        return lax.dot_general(
            left,
            right,
            (((1,), (1,)), ((), ())),
            precision=lax.Precision.HIGHEST,
            preferred_element_type=jnp.float32,
        )
    return lax.dot_general(
        left, right, (((1,), (1,)), ((), ())), preferred_element_type=jnp.float32
    )


def per_device(embeddings, pivots):
    device_count = lax.axis_size(("bank", "sub"))
    my_index = lax.axis_index(("bank", "sub"))
    row_count = embeddings.shape[0]
    start_row = my_index * row_count
    flat_list = pivots.reshape(-1)
    present = (flat_list >= start_row) & (flat_list < start_row + row_count)
    local_index = jnp.clip(flat_list - start_row, 0, row_count - 1)
    picked = jnp.take(embeddings, local_index, axis=0).astype(jnp.float32) * present[
        :, None
    ].astype(jnp.float32)
    chosen = lax.psum(picked, ("bank", "sub")).astype(jnp.bfloat16)
    norms = jnp.einsum("rd,rd->r", embeddings, embeddings, preferred_element_type=jnp.float32)
    chosen_norms = jnp.einsum("rd,rd->r", chosen, chosen, preferred_element_type=jnp.float32)
    dots = times_transposed(embeddings, chosen, False)
    similar = dots / (norms[:, None] + chosen_norms[None, :] - dots)
    block_dots = times_transposed(chosen, chosen, False)
    block = block_dots / (chosen_norms[:, None] + chosen_norms[None, :] - block_dots)
    first_inverse = lower_inverse(jnp.linalg.cholesky(block[:P_SIZE, :P_SIZE]))
    first_factor = times_transposed(similar[:, :P_SIZE], first_inverse, True)
    pivot_first = times_transposed(block[P_SIZE:, :P_SIZE], first_inverse, True)
    second_cols = similar[:, P_SIZE:] - times_transposed(first_factor, pivot_first, True)
    second_block = block[P_SIZE:, P_SIZE:] - times_transposed(pivot_first, pivot_first, True)
    second_inverse = lower_inverse(jnp.linalg.cholesky(second_block))
    second_factor = times_transposed(second_cols, second_inverse, True)
    factor = jnp.concatenate([first_factor, second_factor], axis=1)
    total_rows = row_count * device_count
    local_gram = (
        lax.dot_general(
            factor,
            factor,
            (((0,), (0,)), ((), ())),
            precision=lax.Precision.HIGHEST,
            preferred_element_type=jnp.float32,
        )
        / total_rows
    )
    gram = lax.psum(local_gram, ("bank", "sub"))
    lower_root = jnp.linalg.cholesky(gram)
    basis = times_transposed(factor, lower_inverse(lower_root), True)
    return (basis, lower_root.T)


def solution(mesh):
    in_specs = (P(("bank", "sub"), None), P())
    out_specs = (P(("bank", "sub"), None), P())
    return jax.shard_map(
        per_device, mesh=mesh, in_specs=in_specs, out_specs=out_specs, check_vma=False
    )
```

profile of v0, /device:TPU:2, one launch (start us, length us, event | category | flops | bytes accessed | tf_op | source)
XLA Modules:
  0.0 711.0 jit_solution(15264910173335622265)
XLA Ops:
  7.3 0.7 fusion.81
  8.0 0.7 fusion.79
  8.7 4.1 fusion
  12.8 6.3 gather_fusion
  19.5 87.7 %all-reduce.6 = bf16[512,1024]{1,0:T(8,128)(2,1)S(1)} all-reduce(f32[512,1024]{1,0:T(8,128)S(1)} %convert_multiply_fusion.2), channel_id=1, replica_groups=mesh['bank'=128,'sub'=2] {'bank','sub'}, use_global_device_ids=true, to_apply=%region_0.1 | all-reduce | flops 524288 | bytes 3145728 | tf_op jit(solution)/shard_map/psum | solution.py:39
  107.4 0.8 subtract_divide_fusion.1
  108.4 11.7 %cholesky.357 = f32[128,128]{1,0:T(8,128)S(1)} custom-call(f32[128,128]{1,0:T(8,128)S(1)} %cholesky.407), custom_call_target="Cholesky" | custom-call | tf_op jit(solution)/shard_map/jit(cholesky)/cholesky | solution.py:46
  120.2 9.8 %custom-call.43 = f32[1,128,128]{1,2,0:T(8,128)S(1)} custom-call(f32[1,128,128]{2,1,0:T(8,128)S(1)} %get-tuple-element.80), custom_call_target="InvertDiagBlocksLowerTriangular" | custom-call | tf_op jit(solution)/shard_map/jit(cholesky)/cholesky/custom-call.1 | solution.py:46
  130.5 11.7 %cholesky.367 = f32[128,128]{1,0:T(8,128)S(1)} custom-call(f32[128,128]{1,0:T(8,128)S(1)} %convolution_subtract_fusion.10), custom_call_target="Cholesky" | custom-call | tf_op jit(solution)/shard_map/jit(cholesky)/cholesky | solution.py:46
  142.2 0.7 compare_reduce_fusion.2
  144.2 3.8 while.6
  144.8 1.3 bitcast_dynamic-update-slice_fusion.7
  146.7 1.3 bitcast_dynamic-update-slice_fusion.7
  148.0 20.1 %custom-call.44 = f32[2,128,128]{1,2,0:T(8,128)S(1)} custom-call(f32[2,128,128]{2,1,0:T(8,128)S(1)} %get-tuple-element.27), custom_call_target="InvertDiagBlocksLowerTriangular" | custom-call | tf_op jit(solution)/shard_map/triangular_solve/custom-call.9 | solution.py:11
  170.9 11.7 %cholesky.384 = f32[128,128]{1,0:T(8,128)S(1)} custom-call(f32[128,128]{1,0:T(8,128)S(1)} %cholesky.410), custom_call_target="Cholesky" | custom-call | tf_op jit(solution)/shard_map/jit(cholesky)/cholesky | solution.py:51
  182.7 9.8 %custom-call.45 = f32[1,128,128]{1,2,0:T(8,128)S(1)} custom-call(f32[1,128,128]{2,1,0:T(8,128)S(1)} %get-tuple-element.76), custom_call_target="InvertDiagBlocksLowerTriangular" | custom-call | tf_op jit(solution)/shard_map/jit(cholesky)/cholesky/custom-call.1 | solution.py:51
  193.0 11.7 %cholesky.394 = f32[128,128]{1,0:T(8,128)S(1)} custom-call(f32[128,128]{1,0:T(8,128)S(1)} %convolution_subtract_fusion.9), custom_call_target="Cholesky" | custom-call | tf_op jit(solution)/shard_map/jit(cholesky)/cholesky | solution.py:51
  204.7 0.7 compare_reduce_fusion
  207.3 3.8 while.7
  207.9 1.3 bitcast_dynamic-update-slice_fusion.8
  209.8 1.3 bitcast_dynamic-update-slice_fusion.8
  211.1 19.9 %custom-call.46 = f32[2,128,128]{1,2,0:T(8,128)S(1)} custom-call(f32[2,128,128]{2,1,0:T(8,128)S(1)} %get-tuple-element.28), custom_call_target="InvertDiagBlocksLowerTriangular" | custom-call | tf_op jit(solution)/shard_map/triangular_solve/custom-call.9 | solution.py:11
  231.9 5.7 subtract_divide_fusion
  237.6 3.0 fusion.3
  240.6 3.2 convolution_subtract_fusion
  243.8 3.0 fusion.30
  246.9 1.7 copy-done
  248.5 11.9 %fusion.17 = f32[512,512]{0,1:T(8,128)} fusion(f32[3072,256]{0,1:T(8,128)S(1)} %fusion.30, f32[3072,256]{0,1:T(8,128)S(1)} %fusion.3), kind=kOutput, calls=%fused_computation.50 | convolution fusion | flops 9665511424 | bytes 7340032 | tf_op jit(solution)/shard_map/dot_general | solution.py:56
  260.5 0.8 iota_compare_fusion
  261.3 1.1 fusion.26
  262.4 255.3 %all-reduce.5.cloned.1.call-done = f32[512,512]{0,1:T(8,128)} async-done(((f32[512,512]{0,1:T(8,128)}), f32[512,512]{0,1:T(8,128)}) %all-reduce.5.cloned.1.call-update) | async-done | bytes 1048592 | tf_op jit(solution)/shard_map/psum | solution.py:65
  517.8 2.5 copy.12
  520.3 1.8 fusion.14
  522.1 1.0 copy-done.2
  523.1 11.7 %cholesky.167 = f32[128,128]{1,0:T(8,128)S(1)} custom-call(f32[128,128]{1,0:T(8,128)S(1)} %cholesky.413), custom_call_target="Cholesky" | custom-call | tf_op jit(solution)/shard_map/jit(cholesky)/cholesky | solution.py:66
  534.9 1.1 cholesky.280
  536.0 9.8 %custom-call.35 = f32[1,128,128]{1,2,0:T(8,128)S(1)} custom-call(f32[1,128,128]{2,1,0:T(8,128)S(1)} %get-tuple-element.72), custom_call_target="InvertDiagBlocksLowerTriangular" | custom-call | tf_op jit(solution)/shard_map/jit(cholesky)/cholesky | solution.py:66
  545.8 1.9 constant_dynamic-update-slice_fusion.5
  547.7 1.2 convolution_subtract_fusion.5
  549.0 11.7 %cholesky.190 = f32[128,128]{1,0:T(8,128)S(1)} custom-call(f32[128,128]{1,0:T(8,128)S(1)} %cholesky.417), custom_call_target="Cholesky" | custom-call | tf_op jit(solution)/shard_map/jit(cholesky)/cholesky | solution.py:66
  562.0 0.7 compare_reduce_fusion.7
  562.7 9.9 %custom-call.36 = f32[1,128,128]{1,2,0:T(8,128)S(1)} custom-call(f32[1,128,128]{2,1,0:T(8,128)S(1)} %get-tuple-element.69), custom_call_target="InvertDiagBlocksLowerTriangular" | custom-call | tf_op jit(solution)/shard_map/jit(cholesky)/cholesky | solution.py:66
  572.6 0.9 convolution_dynamic-update-slice_fusion
  573.5 1.5 convolution_subtract_fusion.6
  575.0 11.7 %cholesky.294 = f32[128,128]{1,0:T(8,128)S(1)} custom-call(f32[128,128]{1,0:T(8,128)S(1)} %cholesky.422), custom_call_target="Cholesky" | custom-call | tf_op jit(solution)/shard_map/jit(cholesky)/cholesky | solution.py:66
  587.4 0.7 compare_reduce_fusion.5
  588.1 9.8 %custom-call.47 = f32[1,128,128]{1,2,0:T(8,128)S(1)} custom-call(f32[1,128,128]{2,1,0:T(8,128)S(1)} %get-tuple-element.66), custom_call_target="InvertDiagBlocksLowerTriangular" | custom-call | tf_op jit(solution)/shard_map/jit(cholesky)/cholesky/custom-call.1 | solution.py:66
  597.9 0.8 fusion.6
  598.7 1.4 convolution_subtract_fusion.11
  600.1 11.9 %cholesky.307 = f32[128,128]{1,0:T(8,128)S(1)} custom-call(f32[128,128]{1,0:T(8,128)S(1)} %convolution_subtract_fusion.11), custom_call_target="Cholesky" | custom-call | tf_op jit(solution)/shard_map/jit(cholesky)/cholesky | solution.py:66
  612.7 0.7 compare_reduce_fusion.4
  615.9 2.8 fusion.16
  618.8 13.8 %while.5 = (s32[]{:T(128)}, f32[512,512]{1,0:T(8,128)}, s32[4,2]{0,1:T(2,128)S(1)}, f32[4,128,128]{2,1,0:T(8,128)}, s32[]{:T(128)}) while((s32[]{:T(128)}, f32[512,512]{1,0:T(8,128)}, s32[4,2]{0,1:T(2,128)S(1)}, f32[4,128,128]{2,1,0:T(8,128)}, s32[]{:T(128)}) %tuple.78), condition=%wide.while_cond.1, body=%wide.while_body.1.sunk | while | flops 2 | bytes 132705 | solution.py:11
  619.4 2.8 bitcast_dynamic-update-slice_fusion.6
  622.9 2.8 bitcast_dynamic-update-slice_fusion.6
  626.4 2.8 bitcast_dynamic-update-slice_fusion.6
  629.8 2.7 bitcast_dynamic-update-slice_fusion.6
  632.6 40.1 %custom-call.37 = f32[4,128,128]{1,2,0:T(8,128)S(1)} custom-call(f32[4,128,128]{2,1,0:T(8,128)} %get-tuple-element.20), custom_call_target="InvertDiagBlocksLowerTriangular" | custom-call | tf_op jit(solution)/shard_map/triangular_solve | solution.py:11
  672.7 1.2 fusion.37
  674.0 1.4 convolution_subtract_fusion.2
  675.8 1.4 convolution_subtract_fusion.1
  677.7 1.7 convolution_subtract_fusion.4
  679.8 21.6 %fusion.1 = f32[3072,512]{1,0:T(8,128)} fusion(f32[3072,256]{0,1:T(8,128)S(1)} %copy-done.1, f32[3072,256]{0,1:T(8,128)S(1)} %fusion.3, f32[128,512]{1,0:T(8,128)S(1)} %fusion.50, f32[128,512]{1,0:T(8,128)S(1)} %fusion.51, f32[128,512]{1,0:T(8,128)S(1)} %fusion.53, f32[128,512]{1,0:T(8,128)S(1)} %fusion.37), kind=kOutput, calls=%fused_computation.11 | convolution fusion | flops 9666035712 | bytes 13631488 | tf_op jit(solution)/shard_map/dot_general | solution.py:16
  701.4 2.5 copy.14
  (85 shorter events, 15.3 us)
Async XLA Ops:
  7.2 510.6 %all-reduce.5.cloned.1.call-start = ((), (), s32[]{:S(2)}) async-start(), calls=%async_computation | async-start | bytes 2097152 | tf_op jit(solution)/shard_map/psum | solution.py:65
  7.2 161.2 %copy-start.3 = (f32[256,256]{1,0:T(8,128)}, f32[256,256]{1,0:T(8,128)S(1)}, u32[]{:S(2)}) copy-start(f32[256,256]{1,0:T(8,128)S(1)} %fusion.36) | copy-start | bytes 786436
  168.7 62.2 %copy-start.4 = (f32[256,256]{1,0:T(8,128)S(1)}, f32[256,256]{1,0:T(8,128)}, u32[]{:S(2)}) copy-start(f32[256,256]{1,0:T(8,128)} %copy-done.3) | copy-start | bytes 786436
  169.0 0.7 copy-start.5
  231.9 5.8 copy-start.6
  246.9 1.7 copy-start
  522.1 1.0 copy-start.2
  672.7 7.1 copy-start.1
Sparse Core Ops, SparseCore 0:
  260.6 257.1 all-reduce.4
where the time goes:
time: 716 us; the launch traced here: 711 us
  waiting for transfers between devices  255 us (36%)
  other arithmetic  243 us (34%)
  blocking collectives  87.7 us (12%)
  matrix products  67.7 us (9%)
  local copies, waits for them, and re-layouts  37.6 us (5%)
  between operations  19.8 us (3%)
    psum x1, waiting for transfers between devices, per_device(): gram = lax.psum(local_gram, ('bank', 'sub'))  255 us
    psum x1, blocking collectives, per_device(): chosen = lax.psum(picked, ('bank', 'sub')).astype(jnp.bfloat16)  87.7 us
    another operation x15, other arithmetic, per_device(): lower_root = jnp.linalg.cholesky(gram)  81.3 us
    another operation x7, other arithmetic, lower_inverse(): lax.linalg.triangular_solve(factor, identity, left_side=True, lower=True)  80.1 us
    another operation x7, other arithmetic, per_device(): second_inverse = lower_inverse(jnp.linalg.cholesky(second_block))  34.6 us
    another operation x6, other arithmetic, per_device(): first_inverse = lower_inverse(jnp.linalg.cholesky(block[:P_SIZE, :P_SIZE]))  34 us
    dot_general x6, matrix products, times_transposed(): lax.dot_general(left, right, (((1,), (1,)), ((), ())), precision=lax.Prec...  31.8 us
  transfers between devices with their start and end apart: 1, of which 1 were waited for; matrix products, arithmetic and copies ran while one was open for 0% of the time, Pallas kernels for 0%

commit v1 on v0

--- a/solution.py
+++ b/solution.py
@@ -36,7 +36,7 @@
     picked = jnp.take(embeddings, local_index, axis=0).astype(jnp.float32) * present[
         :, None
     ].astype(jnp.float32)
-    chosen = lax.psum(picked, ("bank", "sub")).astype(jnp.bfloat16)
+    chosen = lax.psum(lax.psum(picked, "sub"), "bank").astype(jnp.bfloat16)
     norms = jnp.einsum("rd,rd->r", embeddings, embeddings, preferred_element_type=jnp.float32)
     chosen_norms = jnp.einsum("rd,rd->r", chosen, chosen, preferred_element_type=jnp.float32)
     dots = times_transposed(embeddings, chosen, False)

time: 716 us -> 1360 us (1.90)
  blocking collectives: 87.7 us -> 701 us
  waiting for transfers between devices: 255 us -> 287 us
    psum x1, blocking collectives: 87.7 us -> 701 us  [per_device(): chosen = lax.psum(lax.psum(picked, 'sub'), 'bank').astype(jnp.bfloat16)]
    psum x0 -> x1, waiting for transfers between devices: none -> 31 us  [per_device(): chosen = lax.psum(lax.psum(picked, 'sub'), 'bank').astype(jnp.bfloat16)]
  transfers between devices with their start and end apart: 1 -> 2, of which waited for: 1 -> 2; matrix products, arithmetic and copies ran while one was open for 0% -> 0% of each run, Pallas kernels for 0% -> 0%
where the time goes in v1:
time: 1360 us
  blocking collectives  701 us (52%)
  waiting for transfers between devices  287 us (21%)
  other arithmetic  244 us (18%)
  matrix products  67.7 us (5%)
  local copies, waits for them, and re-layouts  37.9 us (3%)
  between operations  19.9 us (1%)
    psum x1, blocking collectives, per_device(): chosen = lax.psum(lax.psum(picked, 'sub'), 'bank').astype(jnp.bfloat16)  701 us
    psum x1, waiting for transfers between devices, per_device(): gram = lax.psum(local_gram, ('bank', 'sub'))  256 us
    another operation x15, other arithmetic, per_device(): lower_root = jnp.linalg.cholesky(gram)  81.3 us
    another operation x7, other arithmetic, lower_inverse(): lax.linalg.triangular_solve(factor, identity, left_side=True, lower=True)  80.1 us
    another operation x7, other arithmetic, per_device(): second_inverse = lower_inverse(jnp.linalg.cholesky(second_block))  34.6 us
    another operation x6, other arithmetic, per_device(): first_inverse = lower_inverse(jnp.linalg.cholesky(block[:P_SIZE, :P_SIZE]))  34 us
    dot_general x6, matrix products, times_transposed(): lax.dot_general(left, right, (((1,), (1,)), ((), ())), precision=lax.Prec...  31.8 us
    psum x1, waiting for transfers between devices, per_device(): chosen = lax.psum(lax.psum(picked, 'sub'), 'bank').astype(jnp.bfloat16)  31 us
  transfers between devices with their start and end apart: 2, of which 2 were waited for; matrix products, arithmetic and copies ran while one was open for 0% of the time, Pallas kernels for 0%

profile of v1, /device:TPU:2, one launch (start us, length us, event | category | flops | bytes accessed | tf_op | source)
XLA Modules:
  0.0 1357.8 jit_solution(14624836880842670373)
XLA Ops:
  7.2 0.7 fusion.81
  7.9 0.7 fusion.79
  8.6 6.3 gather_fusion
  15.0 1.6 convert_multiply_fusion.2
  16.7 4.1 fusion
  20.8 31.0 %all-reduce.6.cloned.1.call-done = f32[512,1024]{1,0:T(8,128)} async-done(((f32[512,1024]{1,0:T(8,128)}), f32[512,1024]{1,0:T(8,128)}) %all-reduce.6.cloned.1.call-update) | async-done | bytes 2097168 | tf_op jit(solution)/shard_map/psum | solution.py:39
  51.8 700.8 %all-reduce.9 = bf16[512,1024]{1,0:T(8,128)(2,1)S(1)} all-reduce(f32[512,1024]{1,0:T(8,128)} %all-reduce.6.cloned.1.call-done), channel_id=1, replica_groups=mesh['bank'=128,'sub'=2] {'bank'}, use_global_device_ids=true, to_apply=%region_1.2 | all-reduce | flops 524288 | bytes 3145728 | tf_op jit(solution)/shard_map/psum | solution.py:39
  752.9 0.8 subtract_divide_fusion.1
  753.9 11.7 cholesky.357
  765.7 9.8 custom-call.43
  776.0 11.7 cholesky.367
  789.8 3.9 while.6
  790.4 1.3 bitcast_dynamic-update-slice_fusion.7
  792.4 1.3 bitcast_dynamic-update-slice_fusion.7
  793.8 20.1 %custom-call.44 = f32[2,128,128]{1,2,0:T(8,128)S(1)} custom-call(f32[2,128,128]{2,1,0:T(8,128)S(1)} %get-tuple-element.27), custom_call_target="InvertDiagBlocksLowerTriangular" | custom-call | tf_op jit(solution)/shard_map/triangular_solve/custom-call.9 | solution.py:11
  816.6 11.7 cholesky.384
  828.4 9.8 custom-call.45
  838.7 11.7 cholesky.394
  853.1 3.9 while.7
  853.7 1.3 bitcast_dynamic-update-slice_fusion.8
  855.6 1.3 bitcast_dynamic-update-slice_fusion.8
  857.0 19.9 %custom-call.46 = f32[2,128,128]{1,2,0:T(8,128)S(1)} custom-call(f32[2,128,128]{2,1,0:T(8,128)S(1)} %get-tuple-element.28), custom_call_target="InvertDiagBlocksLowerTriangular" | custom-call | tf_op jit(solution)/shard_map/triangular_solve/custom-call.9 | solution.py:11
  877.8 5.7 subtract_divide_fusion
  883.5 3.0 fusion.3
  886.5 3.2 convolution_subtract_fusion
  889.8 3.0 fusion.30
  892.8 1.7 copy-done
  894.4 11.9 fusion.17
  906.4 0.8 iota_compare_fusion
  907.2 1.1 fusion.26
  908.4 256.2 %all-reduce.8.cloned.1.call-done = f32[512,512]{0,1:T(8,128)} async-done(((f32[512,512]{0,1:T(8,128)}), f32[512,512]{0,1:T(8,128)}) %all-reduce.8.cloned.1.call-update) | async-done | bytes 1048592 | tf_op jit(solution)/shard_map/psum | solution.py:65
  1164.6 2.5 copy.12
  1167.1 1.8 fusion.14
  1168.9 1.0 copy-done.2
  1169.9 11.7 cholesky.167
  1181.7 1.1 cholesky.280
  1182.8 9.8 custom-call.35
  1192.6 1.9 constant_dynamic-update-slice_fusion.5
  1194.5 1.2 convolution_subtract_fusion.5
  1195.8 11.7 cholesky.190
  1208.8 0.7 compare_reduce_fusion.7
  1209.5 9.9 custom-call.36
  1219.4 0.9 convolution_dynamic-update-slice_fusion
  1220.4 1.5 convolution_subtract_fusion.6
  1221.8 11.7 cholesky.294
  1234.2 0.7 compare_reduce_fusion.5
  1234.9 9.8 custom-call.47
  1244.7 0.8 fusion.6
  1245.5 1.4 convolution_subtract_fusion.11
  1246.9 11.9 cholesky.307
  1259.5 0.7 compare_reduce_fusion.4
  1262.8 2.8 fusion.16
  1265.6 13.8 %while.5 = (s32[]{:T(128)}, f32[512,512]{1,0:T(8,128)}, s32[4,2]{0,1:T(2,128)S(1)}, f32[4,128,128]{2,1,0:T(8,128)}, s32[]{:T(128)}) while((s32[]{:T(128)}, f32[512,512]{1,0:T(8,128)}, s32[4,2]{0,1:T(2,128)S(1)}, f32[4,128,128]{2,1,0:T(8,128)}, s32[]{:T(128)}) %tuple.78), condition=%wide.while_cond.1, body=%wide.while_body.1.sunk | while | flops 2 | bytes 132705 | solution.py:11
  1266.2 2.8 bitcast_dynamic-update-slice_fusion.6
  1269.7 2.8 bitcast_dynamic-update-slice_fusion.6
  1273.2 2.8 bitcast_dynamic-update-slice_fusion.6
  1276.7 2.7 bitcast_dynamic-update-slice_fusion.6
  1279.4 40.1 %custom-call.37 = f32[4,128,128]{1,2,0:T(8,128)S(1)} custom-call(f32[4,128,128]{2,1,0:T(8,128)} %get-tuple-element.20), custom_call_target="InvertDiagBlocksLowerTriangular" | custom-call | tf_op jit(solution)/shard_map/triangular_solve | solution.py:11
  1319.6 1.2 fusion.37
  1320.8 1.4 convolution_subtract_fusion.2
  1322.6 1.4 convolution_subtract_fusion.1
  1324.5 1.7 convolution_subtract_fusion.4
  1326.6 21.6 %fusion.1 = f32[3072,512]{1,0:T(8,128)} fusion(f32[3072,256]{0,1:T(8,128)S(1)} %copy-done.1, f32[3072,256]{0,1:T(8,128)S(1)} %fusion.3, f32[128,512]{1,0:T(8,128)S(1)} %fusion.50, f32[128,512]{1,0:T(8,128)S(1)} %fusion.51, f32[128,512]{1,0:T(8,128)S(1)} %fusion.53, f32[128,512]{1,0:T(8,128)S(1)} %fusion.37), kind=kOutput, calls=%fused_computation.11 | convolution fusion | flops 9666035712 | bytes 13631488 | tf_op jit(solution)/shard_map/dot_general | solution.py:16
  1348.2 2.5 copy.14
  (84 shorter events, 16.4 us)
Async XLA Ops:
  7.2 44.7 %all-reduce.6.cloned.1.call-start = ((), (), s32[]{:S(2)}) async-start(), calls=%async_computation | async-start | bytes 4194304 | tf_op jit(solution)/shard_map/psum | solution.py:39
  16.6 1148.0 %all-reduce.8.cloned.1.call-start = ((), (), s32[]{:S(2)}) async-start(), calls=%async_computation.1 | async-start | bytes 2097152 | tf_op jit(solution)/shard_map/psum | solution.py:65
  814.7 0.7 copy-start.3
  877.8 5.7 copy-start.4
  892.8 1.7 copy-start
  1168.9 1.0 copy-start.2
  1319.5 7.1 copy-start.1
Sparse Core Ops, SparseCore 0:
  16.7 35.0 all-reduce.5
  906.5 258.0 all-reduce.7
